TPU v7x, 256 devices: a whole 4x4x8 slice. The times are simulated.
256 devices in a mesh: mem: 32 (over y, z), lev: 8 (over x, core).
Axes of the slice: x: 4, y: 4, z: 8, core: 2. Of those that a mesh axis runs over, the one named last changes fastest.
Arguments:
- prior_ensemble_stack: float32 [64, 40, 64, 512], P('mem', 'lev'), may hold values from -6 to 6
- vertical_cfl_ratio: float32 [40, 64, 512], P('lev'), may hold values from -0.35 to 0.35
- horizontal_cfl_ratio: float32 [40, 64, 512], P('lev'), may hold values from -0.35 to 0.35
- spreading_coefficient: float32 [40], P('lev'), may hold values from 0.02 to 0.2
- obs_cells: int32 [2, 16], replicated, may hold values from 0 to 32767
- obs_slabs: int32 [2, 16], replicated, may hold values from 0 to 39
- obs_values: float32 [2, 16], replicated, may hold values from -6 to 6
- obs_error: float32 [2, 16], replicated, may hold values from 0.25 to 2
Outputs:
- analysis: float32 [64, 40, 64, 512], P('mem', 'lev')
All inputs are finite; a program needn't handle non-finite values.
Results may differ from a plain program's by a relative error of at most 0.0001.
Values sent between devices are 32-bit elements; how exact they have to be, the bound alone decides.
A program may use at most 256 MiB of HBM per device.

v0:
```python
import jax
import jax.numpy as jnp
from jax import lax
from jax.sharding import PartitionSpec as P

NX = 512
STEPS = 2
LOC_HALF = 64


def predicted_model_vector(
    ensemble_gridded_values, vertical_cfl_ratio, horizontal_cfl_ratio, spreading_coefficient
):
    diffuse = spreading_coefficient[:, None, None]
    for time_step in range(STEPS):
        widths = [(0, 0)] * (ensemble_gridded_values.ndim - 2) + [(1, 1), (1, 1)]
        padded = jnp.pad(ensemble_gridded_values, widths, mode="edge")
        east_cell = padded[..., 1:-1, 2:]
        west_cell = padded[..., 1:-1, :-2]
        north_cell = padded[..., 2:, 1:-1]
        south_cell = padded[..., :-2, 1:-1]
        ensemble_gridded_values = (
            ensemble_gridded_values
            - 0.5 * vertical_cfl_ratio * (east_cell - west_cell)
            - 0.5 * horizontal_cfl_ratio * (north_cell - south_cell)
            + diffuse
            * (east_cell + west_cell + north_cell + south_cell - 4.0 * ensemble_gridded_values)
        )
    return ensemble_gridded_values


def grid_distance(cells_a, cells_b):
    row_gap = (cells_a[:, None] // NX - cells_b[None, :] // NX).astype(jnp.float32)
    col_gap = (cells_a[:, None] % NX - cells_b[None, :] % NX).astype(jnp.float32)
    return jnp.sqrt(row_gap * row_gap + col_gap * col_gap)


def gaspari_taper(dist):
    scaled = dist / LOC_HALF
    inner_portion = (
        ((-0.25 * scaled + 0.5) * scaled + 0.625) * scaled - 5.0 / 3.0
    ) * scaled * scaled + 1.0
    safe_ratio = jnp.maximum(scaled, 1.0)
    outer_portion = (
        ((((scaled / 12.0 - 0.5) * scaled + 0.625) * scaled + 5.0 / 3.0) * scaled - 5.0) * scaled
        + 4.0
        - 2.0 / (3.0 * safe_ratio)
    )
    return jnp.where(scaled <= 1.0, inner_portion, jnp.where(scaled < 2.0, outer_portion, 0.0))


def obs_space(prior_rows, row_cells, first_row, obs_cell, obs_value, obs_var):
    member_count = prior_rows.shape[1]
    reach_table = gaspari_taper(grid_distance(row_cells, obs_cell))

    def advance_obs(current, position):
        own_row = lax.dynamic_index_in_dim(current, first_row + position, 0, False)
        row_mean = jnp.mean(own_row)
        anomaly = own_row - row_mean
        spread = jnp.sum(anomaly * anomaly) / (member_count - 1) + 1e-06
        error_var = lax.dynamic_index_in_dim(obs_var, position, 0, False)
        seen_value = lax.dynamic_index_in_dim(obs_value, position, 0, False)
        shrink = jnp.sqrt(error_var / (spread + error_var))
        increment = (
            (row_mean * error_var + seen_value * spread) / (spread + error_var)
            - row_mean
            + (shrink - 1.0) * anomaly
        )
        centered = current - jnp.mean(current, axis=1, keepdims=True)
        slopes = jnp.dot(centered, anomaly, precision=lax.Precision.HIGHEST) / (
            (member_count - 1) * spread
        )
        weight = lax.dynamic_index_in_dim(reach_table, position, 1, False)
        current = current + (weight * slopes)[:, None] * increment[None, :]
        return (current, (anomaly, spread, increment))

    positions = jnp.arange(obs_cell.shape[0], dtype=jnp.int32)
    prior_rows, obs_plan = lax.scan(advance_obs, prior_rows, positions)
    return (obs_plan, prior_rows)


def settle(state_rows, obs_plan, cell_loc):
    prior_anoms, spreads, increments = obs_plan
    member_count = state_rows.shape[0]
    centered = state_rows - jnp.mean(state_rows, axis=0, keepdims=True)
    cross_cov = jnp.einsum(
        "km,msc->ksc", prior_anoms, centered, precision=lax.Precision.HIGHEST
    ) / (member_count - 1)
    incr_anom = increments - jnp.mean(increments, axis=1, keepdims=True)
    incr_link = jnp.dot(incr_anom, prior_anoms.T, precision=lax.Precision.HIGHEST) / (
        member_count - 1
    )

    def solve_step(weights, position):
        column = lax.dynamic_index_in_dim(incr_link, position, 1, False)
        summed_total = lax.dynamic_index_in_dim(cross_cov, position, 0, False) + jnp.einsum(
            "j,jsc->sc", column, weights, precision=lax.Precision.HIGHEST
        )
        taper_row = lax.dynamic_index_in_dim(cell_loc, position, 0, False)
        update_row = (
            taper_row[None, :]
            * summed_total
            / lax.dynamic_index_in_dim(spreads, position, 0, False)
        )
        return (lax.dynamic_update_index_in_dim(weights, update_row, position, 0), None)

    positions = jnp.arange(cross_cov.shape[0], dtype=jnp.int32)
    weights, unused = lax.scan(solve_step, jnp.zeros_like(cross_cov), positions)
    return state_rows + jnp.einsum(
        "km,ksc->msc", increments, weights, precision=lax.Precision.HIGHEST
    )


def pick_rows(state_rows, obs_slab, obs_cell, slab_base, cell_base):
    slab_dev = state_rows.shape[1]
    cell_dev = state_rows.shape[2]
    slab_off = obs_slab - slab_base
    cell_off = obs_cell - cell_base
    inside = (slab_off >= 0) & (slab_off < slab_dev) & (cell_off >= 0) & (cell_off < cell_dev)
    taken_rows = state_rows[
        :, jnp.clip(slab_off, 0, slab_dev - 1), jnp.clip(cell_off, 0, cell_dev - 1)
    ]
    return jnp.where(inside[:, None], taken_rows.T, 0.0)


def body(
    prior_ensemble_stack,
    vertical_cfl_ratio,
    horizontal_cfl_ratio,
    spreading_coefficient,
    obs_cells,
    obs_slabs,
    obs_values,
    obs_error,
):
    mem_dev, slab_dev, grid_rows, grid_cols = prior_ensemble_stack.shape
    cell_total = grid_rows * grid_cols
    cell_dev = cell_total // lax.axis_size("mem")
    batch_count = obs_cells.shape[0]
    ensemble_gridded_values = predicted_model_vector(
        prior_ensemble_stack, vertical_cfl_ratio, horizontal_cfl_ratio, spreading_coefficient
    )
    by_cells = ensemble_gridded_values.reshape(mem_dev, slab_dev, cell_total)
    cell_base = lax.axis_index("mem") * cell_dev
    slab_base = lax.axis_index("lev") * slab_dev
    local_cells = cell_base + jnp.arange(cell_dev, dtype=jnp.int32)
    cell_locs = [
        gaspari_taper(grid_distance(obs_cells[batch_no], local_cells))
        for batch_no in range(batch_count)
    ]
    state_rows = lax.all_to_all(by_cells, "mem", split_axis=2, concat_axis=0, tiled=True)
    for batch_no in range(batch_count):
        partial_value = pick_rows(
            state_rows, obs_slabs[batch_no], obs_cells[batch_no], slab_base, cell_base
        )
        prior_rows = lax.psum(partial_value, ("mem", "lev"))
        obs_plan, carried = obs_space(
            prior_rows,
            obs_cells[batch_no],
            0,
            obs_cells[batch_no],
            obs_values[batch_no],
            obs_error[batch_no],
        )
        state_rows = settle(state_rows, obs_plan, cell_locs[batch_no])
    result = lax.all_to_all(state_rows, "mem", split_axis=0, concat_axis=2, tiled=True)
    return result.reshape(prior_ensemble_stack.shape)


def solution(mesh):
    in_specs = (
        P("mem", "lev", None, None),
        P("lev", None, None),
        P("lev", None, None),
        P("lev"),
        P(),
        P(),
        P(),
        P(),
    )
    out_specs = P("mem", "lev", None, None)
    return jax.shard_map(body, mesh=mesh, in_specs=in_specs, out_specs=out_specs, check_vma=False)
```

profile of v0, /device:TPU:32, one launch (start us, length us, event | category | flops | bytes accessed | tf_op | source)
XLA Modules:
  0.0 885.0 jit_solution(8341985732564809340)
XLA Ops:
  0.0 1.0 fusion.104
  1.1 1.5 broadcast_multiply_fusion.2
  2.7 2.2 multiply_add_fusion.5
  5.0 2.2 multiply_add_fusion.4
  7.2 22.3 %copy.56 = f32[2,5,64,512]{1,0,3,2:T(2,128)} copy(f32[2,5,64,512]{3,2,1,0:T(8,128)S(1)} %multiply_add_fusion.4) | data formatting | bytes 2621440 | tf_op jit(solution)/shard_map/reshape | solution.py:143
  29.5 46.4 %reshape.447 = f32[32,1,10240]{2,1,0:T(1,128)} reshape(f32[32768,2,5]{2,1,0:T(2,128)} %bitcast.261) | data formatting | bytes 2621440
  75.9 11.5 %all-to-all-start = ((f32[32,1,10240]{2,1,0:T(1,128)}), f32[32,1,10240]{2,1,0:T(1,128)S(1)}, u32[]{:S(2)}, u32[]{:S(2)}) async-start(f32[32,1,10240]{2,1,0:T(1,128)} %reshape.447), calls=%async_computation | async-start | bytes 2621440 | tf_op jit(solution)/shard_map/all_to_all | solution.py:151
  88.1 33.2 %all-to-all-done = f32[32,1,10240]{2,1,0:T(1,128)S(1)} async-done(((f32[32,1,10240]{2,1,0:T(1,128)}), f32[32,1,10240]{2,1,0:T(1,128)S(1)}, u32[]{:S(2)}, u32[]{:S(2)}) %all-to-all-start) | async-done | bytes 1310752 | tf_op jit(solution)/shard_map/all_to_all | solution.py:151
  121.9 3.8 reduce.3
  125.6 65.2 %reshape.448 = f32[32768,2,5]{2,1,0:T(2,128)} reshape(f32[32,10240]{1,0:T(8,128)S(1)} %reduce.3) | data formatting | bytes 2621440
  190.8 26.8 %copy.55 = f32[2,5,32,1024]{3,2,0,1:T(8,128)S(1)} copy(f32[2,5,32,1024]{1,0,3,2:T(2,128)} %bitcast.262) | data formatting | bytes 2621440 | tf_op jit(solution)/shard_map/all_to_all | solution.py:151
  217.7 2.1 copy.38
  219.8 2.2 all_to_all.27
  222.0 2.0 copy.39
  224.0 1.6 gather_fusion
  225.7 74.7 %psum.14 = f32[16,64]{1,0:T(8,128)S(1)} all-reduce(f32[16,64]{1,0:T(8,128)S(1)} %broadcast_select_fusion.1), channel_id=1, replica_groups=mesh['mem'=32,'lev'=8] {'mem','lev'}, use_global_device_ids=true, to_apply=%region_0.1 | all-reduce | flops 1024 | bytes 8192 | tf_op jit(solution)/shard_map/psum | solution.py:156
  300.4 152.3 %while.56 = (s32[]{:T(128)}, f32[16,64]{1,0:T(8,128)S(1)}, f32[16,64]{1,0:T(8,128)S(1)}, f32[16]{0:T(128)S(1)}, f32[16,64]{1,0:T(8,128)S(1)}, /*index=5*/s32[16]...) while((s32[]{:T(128)}, f32[16,64]{1,0:T(8,128)S(1)}, ...), condition=%wide.region_5.6_spmd, body=%wide.region_1.5_spmd.sunk | while | flops 16943 | bytes 20615 | solution.py:78
  453.1 0.8 fusion.50
  454.0 69.2 %while.57 = (s32[]{:T(128)}, f32[16,5,1024]{2,1,0:T(8,128)S(1)}, s32[16]{0:T(128)S(1)}, f32[16,1024]{1,0:T(8,128)S(1)}, f32[16,5,1024]{2,0,1:T(8,128)S(1)}, /*in...) while((s32[]{:T(128)}, f32[16,5,1024]{2,1,0:T(8,128)S(1)}, ...), condition=%wide.region_9.10_spmd, body=%wide.region_8.9_spmd.sunk | while | flops 998405 | bytes 672435 | solution.py:108
  457.6 0.7 fusion.139
  461.9 0.7 fusion.139
  466.3 0.7 fusion.139
  470.6 0.7 fusion.139
  474.9 0.7 fusion.139
  479.2 0.7 fusion.139
  483.6 0.7 fusion.139
  487.9 0.7 fusion.139
  492.2 0.7 fusion.139
  496.5 0.7 fusion.139
  500.9 0.7 fusion.139
  505.2 0.7 fusion.139
  509.5 0.7 fusion.139
  513.8 0.7 fusion.139
  518.2 0.7 fusion.139
  523.2 1.3 fusion.105
  524.5 2.0 copy.43
  526.5 1.6 gather_fusion.1
  528.2 72.6 %psum.15 = f32[16,64]{1,0:T(8,128)S(1)} all-reduce(f32[16,64]{1,0:T(8,128)S(1)} %broadcast_select_fusion), channel_id=1, replica_groups=mesh['mem'=32,'lev'=8] {'mem','lev'}, use_global_device_ids=true, to_apply=%region_10.11 | all-reduce | flops 1024 | bytes 8192 | tf_op jit(solution)/shard_map/psum | solution.py:156
  600.7 152.3 %while.58 = (s32[]{:T(128)}, f32[16,64]{1,0:T(8,128)S(1)}, f32[16,64]{1,0:T(8,128)S(1)}, f32[16]{0:T(128)S(1)}, f32[16,64]{1,0:T(8,128)S(1)}, /*index=5*/s32[16]...) while((s32[]{:T(128)}, f32[16,64]{1,0:T(8,128)S(1)}, ...), condition=%wide.region_15.16_spmd, body=%wide.region_11.15_spmd.sunk | while | flops 16943 | bytes 20615 | solution.py:78
  753.5 0.8 fusion.53
  754.3 69.2 %while.59 = (s32[]{:T(128)}, f32[16,5,1024]{2,1,0:T(8,128)S(1)}, s32[16]{0:T(128)S(1)}, f32[16,1024]{1,0:T(8,128)S(1)}, f32[16,5,1024]{2,0,1:T(8,128)S(1)}, /*in...) while((s32[]{:T(128)}, f32[16,5,1024]{2,1,0:T(8,128)S(1)}, ...), condition=%wide.region_19.20_spmd, body=%wide.region_18.19_spmd.sunk | while | flops 998405 | bytes 672435 | solution.py:108
  814.2 0.7 fusion.149
  822.9 0.7 fusion.149
  823.5 1.3 convolution_add_fusion
  824.8 0.8 copy.47
  825.6 57.4 %all_to_all.33 = f32[64,5,1024]{2,1,0:T(8,128)S(1)} all-to-all(f32[64,5,1024]{2,1,0:T(8,128)S(1)} %copy.47), channel_id=1, replica_groups=mesh['mem'=32,'lev'=8] {'mem'}, dimensions={0} | all-to-all | bytes 2621440 | tf_op jit(solution)/shard_map/all_to_all | solution.py:166
  883.0 0.8 copy.48
  883.8 1.3 reshape.421
  (675 shorter events, 180.0 us)
Async XLA Ops:
  1.0 1.7 copy-start
  1.0 1.7 copy-start.3
  75.9 11.5 %copy-start.1 = (s32[2,16]{1,0:T(2,128)S(1)}, s32[2,16]{1,0:T(2,128)}, u32[]{:S(2)}) copy-start(s32[2,16]{1,0:T(2,128)} %param.20) | copy-start | bytes 388
  75.9 11.7 %copy-start.2 = (s32[2,16]{1,0:T(2,128)S(1)}, s32[2,16]{1,0:T(2,128)}, u32[]{:S(2)}) copy-start(s32[2,16]{1,0:T(2,128)} %param.21) | copy-start | bytes 388
  75.9 11.7 %copy-start.4 = (f32[2,16]{1,0:T(2,128)S(1)}, f32[2,16]{1,0:T(2,128)}, u32[]{:S(2)}) copy-start(f32[2,16]{1,0:T(2,128)} %param.22) | copy-start | bytes 388
  75.9 11.7 %copy-start.5 = (f32[2,16]{1,0:T(2,128)S(1)}, f32[2,16]{1,0:T(2,128)}, u32[]{:S(2)}) copy-start(f32[2,16]{1,0:T(2,128)} %param.23) | copy-start | bytes 388
  75.9 45.4 %all-to-all-start = ((f32[32,1,10240]{2,1,0:T(1,128)}), f32[32,1,10240]{2,1,0:T(1,128)S(1)}, u32[]{:S(2)}, u32[]{:S(2)}) async-start(f32[32,1,10240]{2,1,0:T(1,128)} %reshape.447), calls=%async_computation | async-start | bytes 2621440 | tf_op jit(solution)/shard_map/all_to_all | solution.py:151
where the time goes:
time: 890 us; the launch traced here: 885 us
  local copies, waits for them, and re-layouts  278 us (31%)
  loops' own time  254 us (29%)
  blocking collectives  205 us (23%)
  other arithmetic  77.4 us (9%)
  waiting for transfers between devices  33.2 us (4%)
  matrix products  25.7 us (3%)
  starting transfers between devices  11.5 us (1%)
    another operation x2, loops' own time, obs_space(): prior_rows, obs_plan = lax.scan(advance_obs, prior_rows, positions)  191 us
    psum x2, blocking collectives, body(): prior_rows = lax.psum(partial_value, ('mem', 'lev'))  147 us
    unnamed x14, local copies, waits for them, and re-layouts  112 us
    another operation x2, loops' own time, settle(): weights, unused = lax.scan(solve_step, jnp.zeros_like(cross_cov), positions)  63.7 us
    all_to_all x1, blocking collectives, body(): lax.all_to_all(state_rows, 'mem', split_axis=0, concat_axis=2, tiled=True)  57.4 us
    dynamic_slice x64, local copies, waits for them, and re-layouts, obs_space(): prior_rows, obs_plan = lax.scan(advance_obs, prior_rows, positions)  37.4 us
    all_to_all x5, local copies, waits for them, and re-layouts, body(): lax.all_to_all(by_cells, 'mem', split_axis=2, concat_axis=0, tiled=True)  33.6 us
    all_to_all x1, waiting for transfers between devices, body(): lax.all_to_all(by_cells, 'mem', split_axis=2, concat_axis=0, tiled=True)  33.2 us
  transfers between devices with their start and end apart: 1, of which 1 were waited for; matrix products, arithmetic and copies ran while one was open for 0% of the time, Pallas kernels for 0%

commit v1 on v0

v1 whole, which is shorter than its diff:
```python
import functools

import jax
import jax.numpy as jnp
from jax import lax
from jax.experimental import pallas as pl
from jax.experimental.pallas import tpu as pltpu
from jax.sharding import PartitionSpec as P

NX = 512
STEPS = 2
LOC_HALF = 64
MESH = pl.DeviceIdType.MESH
ROWS, LANES = 8, 128
EARLY = 2


def taper(dist):
    scaled = dist * (1.0 / LOC_HALF)
    inner = (
        ((-0.25 * scaled + 0.5) * scaled + 0.625) * scaled - 5.0 / 3.0
    ) * scaled * scaled + 1.0
    safe = jnp.maximum(scaled, 1.0)
    outer = (
        ((((scaled * (1.0 / 12.0) - 0.5) * scaled + 0.625) * scaled + 5.0 / 3.0) * scaled - 5.0)
        * scaled
        + 4.0
        - 2.0 / (3.0 * safe)
    )
    return jnp.where(scaled <= 1.0, inner, jnp.where(scaled < 2.0, outer, 0.0))


def kernel(
    n_mem,
    n_lev,
    prior,
    vert,
    horz,
    diff,
    cells,
    slabs,
    vals,
    errs,
    out,
    pin,
    vin,
    hin,
    coef,
    field,
    blocks,
    got_lev,
    got_mem,
    msg,
    picked,
    square,
    anom,
    mean,
    obs_loc,
    place,
    plan,
    table,
    cell_loc,
    push,
    in_sem,
    lev_send,
    lev_recv,
    mem_send,
    mem_recv,
    out_send,
    out_recv,
    back_send,
    back_recv,
    plan_sem,
    own_sem,
):
    mem_dev, n_slab, grid_rows, grid_cols = prior.shape
    n_batch, n_per = cells.shape
    n_obs = n_batch * n_per
    members = mem_dev * n_mem
    half = LANES // mem_dev
    tiles_across = grid_cols // LANES
    me = lax.axis_index("mem")
    lev = lax.axis_index("lev")
    tile_row, tile_col = me // tiles_across, me % tiles_across

    def tile_of(ref, lead, d):
        r = pl.multiple_of((d // tiles_across) * ROWS, ROWS)
        c = pl.multiple_of((d % tiles_across) * LANES, LANES)
        return ref.at[lead + (pl.ds(r, ROWS), pl.ds(c, LANES))]

    def fetch(s):
        return (
            pltpu.make_async_copy(prior.at[:, s], pin.at[s], in_sem.at[0, s]),
            pltpu.make_async_copy(vert.at[s], vin.at[s], in_sem.at[1, s]),
            pltpu.make_async_copy(horz.at[s], hin.at[s], in_sem.at[2, s]),
        )

    @pl.loop(0, n_slab)
    def _(s):
        for copy in fetch(s):
            copy.start()

    barrier = pltpu.get_barrier_semaphore()

    @pl.loop(1, n_mem)
    def _(i):
        pl.semaphore_signal(
            barrier, inc=1, device_id={"mem": lax.rem(me + i, n_mem)}, device_id_type=MESH
        )

    @pl.loop(1, n_lev)
    def _(i):
        pl.semaphore_signal(
            barrier, inc=1, device_id={"lev": lax.rem(lev + i, n_lev)}, device_id_type=MESH
        )

    col = lax.broadcasted_iota(jnp.int32, (grid_rows, grid_cols), 1)
    row = lax.broadcasted_iota(jnp.int32, (grid_rows, grid_cols), 0)

    def forecast(s):
        for copy in fetch(s):
            copy.wait()
        d = diff[s]
        v = 0.5 * vin[s]
        h = 0.5 * hin[s]
        coef[0] = d - v
        coef[1] = d + v
        coef[2] = d - h
        coef[3] = d + h
        centre = 1.0 - 4.0 * d

        @pl.loop(0, mem_dev)
        def _(p):
            f = pin[s, p]
            for _step in range(STEPS):
                east = jnp.where(col == grid_cols - 1, f, pltpu.roll(f, grid_cols - 1, 1))
                west = jnp.where(col == 0, f, pltpu.roll(f, 1, 1))
                north = jnp.where(row == grid_rows - 1, f, pltpu.roll(f, grid_rows - 1, 0))
                south = jnp.where(row == 0, f, pltpu.roll(f, 1, 0))
                f = (
                    centre * f
                    + (coef[0] * east + coef[1] * west)
                    + (coef[2] * north + coef[3] * south)
                )
            field[s, p] = f

    def send_blocks(s):
        for p in range(mem_dev):
            blocks[s, me, p] = field[
                s,
                p,
                pl.ds(pl.multiple_of(tile_row * ROWS, ROWS), ROWS),
                pl.ds(pl.multiple_of(tile_col * LANES, LANES), LANES),
            ]

        @pl.loop(1, n_mem)
        def _(i):
            d = lax.rem(me + i, n_mem)
            pltpu.make_async_remote_copy(
                src_ref=tile_of(field, (s, slice(None)), d),
                dst_ref=blocks.at[s, me],
                send_sem=out_send.at[s],
                recv_sem=out_recv.at[s],
                device_id={"mem": d},
                device_id_type=MESH,
            ).start()

    forecast(0)
    pl.semaphore_wait(barrier, n_mem - 1 + n_lev - 1)
    send_blocks(0)

    @pl.loop(1, EARLY)
    def _(s):
        forecast(s)
        send_blocks(s)

    @pl.loop(EARLY, n_slab)
    def _(s):
        forecast(s)

    lane512 = lax.broadcasted_iota(jnp.int32, (1, grid_cols), 1)

    @pl.loop(0, n_obs)
    def _(k):
        b, q = k // n_per, lax.rem(k, n_per)
        cell = cells[b, q]
        at_row, at_col = lax.shift_right_logical(cell, 9), jnp.bitwise_and(cell, NX - 1)
        off = slabs[b, q] - lev * n_slab
        inside = jnp.logical_and(off >= 0, off < n_slab)
        wanted = jnp.where(inside, at_col, -1)
        near = jnp.clip(off, 0, n_slab - 1)
        for p in range(mem_dev):
            line = field[near, p, pl.ds(at_row, 1), :]
            line = jnp.where(lane512 == wanted, line, 0.0)
            total = line[:, :LANES]
            for t in range(1, tiles_across):
                total = total + line[:, t * LANES : (t + 1) * LANES]
            picked[p, pl.ds(k, 1), :] = total
        place[0, pl.ds(k, 1), :] = jnp.full((1, LANES), at_row.astype(jnp.float32))
        place[1, pl.ds(k, 1), :] = jnp.full((1, LANES), at_col.astype(jnp.float32))

    sub32 = lax.broadcasted_iota(jnp.int32, (n_obs, LANES), 0)
    lane32 = lax.broadcasted_iota(jnp.int32, (n_obs, LANES), 1)
    share = jnp.zeros((1, LANES), jnp.float32)
    for p in range(mem_dev):
        column = jnp.sum(picked[p], axis=1, keepdims=True)
        share = share + jnp.sum(
            jnp.where(lane32 == sub32 + p * half, column, 0.0), axis=0, keepdims=True
        )
    msg[0] = share
    got_lev[lev] = share

    @pl.loop(1, n_lev)
    def _(i):
        pltpu.make_async_remote_copy(
            src_ref=msg.at[0],
            dst_ref=got_lev.at[lev],
            send_sem=lev_send,
            recv_sem=lev_recv,
            device_id={"lev": lax.rem(lev + i, n_lev)},
            device_id_type=MESH,
        ).start()

    cell_row = (
        tile_row * ROWS + lax.broadcasted_iota(jnp.int32, (ROWS, LANES), 0)
    ).astype(jnp.float32)
    cell_col = (
        tile_col * LANES + lax.broadcasted_iota(jnp.int32, (ROWS, LANES), 1)
    ).astype(jnp.float32)

    def lev_rows(copies):
        return got_lev.at[pl.ds(0, copies)]

    pltpu.make_async_copy(lev_rows(n_lev - 1), lev_rows(n_lev - 1), lev_recv).wait()
    total = got_lev[0]
    for i in range(1, n_lev):
        total = total + got_lev[i]
    msg[1] = total
    got_mem[me] = total

    @pl.loop(1, n_mem)
    def _(i):
        pltpu.make_async_remote_copy(
            src_ref=msg.at[1],
            dst_ref=got_mem.at[me],
            send_sem=mem_send,
            recv_sem=mem_recv,
            device_id={"mem": lax.rem(me + i, n_mem)},
            device_id_type=MESH,
        ).start()

    @pl.loop(EARLY, n_slab)
    def _(s):
        send_blocks(s)

    @pl.loop(0, n_obs)
    def _(k):
        b, q = k // n_per, lax.rem(k, n_per)
        cell = cells[b, q]
        r = lax.shift_right_logical(cell, 9).astype(jnp.float32)
        c = jnp.bitwise_and(cell, NX - 1).astype(jnp.float32)
        dr, dc = place[0] - r, place[1] - c
        obs_loc[k] = taper(jnp.sqrt(dr * dr + dc * dc))
        dr, dc = cell_row - r, cell_col - c
        cell_loc[k] = taper(jnp.sqrt(dr * dr + dc * dc))

    square[...] = jnp.zeros_like(square)
    pltpu.make_async_copy(
        got_mem.at[pl.ds(0, n_mem - 1)], got_mem.at[pl.ds(0, n_mem - 1)], mem_recv
    ).wait()

    @pl.loop(0, n_mem)
    def _(i):
        square[pl.ds(i, 1), :] = got_mem[i]

    turned = square[...].T
    rows = turned[:n_obs]
    for p in range(1, mem_dev):
        rows = rows + pltpu.roll(turned[p * half : p * half + n_obs], p * half, 1)
    rows_mean = jnp.sum(rows, axis=1, keepdims=True) * (1.0 / members)
    used = lax.rem(lane32, half) < n_mem
    anom[...] = jnp.where(used, rows - rows_mean, 0.0)
    mean[...] = jnp.broadcast_to(rows_mean, (n_obs, LANES))
    lane1 = lax.broadcasted_iota(jnp.int32, (1, LANES), 1)

    @pl.loop(0, n_obs)
    def _(k):
        b, q = k // n_per, lax.rem(k, n_per)
        r, o = errs[b, q], vals[b, q]
        a = anom[pl.ds(k, 1), :]
        m = mean[pl.ds(k, 1), :]
        every = anom[...]
        g = jnp.sum(every * a, axis=1, keepdims=True)
        v = jnp.sum(a * a, axis=1, keepdims=True) * (1.0 / (members - 1)) + 1e-06
        v = jnp.broadcast_to(v, (1, LANES))
        inv = 1.0 / (v + r)
        less = jnp.sqrt(r * inv) - 1.0
        move = (m * r + o * v) * inv - m
        gain = 1.0 / ((members - 1) * v)
        c = obs_loc[k] * g * gain
        anom[...] = every + (c * less) * a
        mean[...] = mean[...] + c * move
        plan[pl.ds(k, 1), :] = a
        plan[pl.ds(2 * n_obs + k, 1), :] = jnp.where(
            lane1 == 0, less, jnp.where(lane1 == 1, move, gain)
        )

    y = plan[:n_obs]
    link = lax.dot_general(
        y,
        y,
        (((1,), (1,)), ((), ())),
        precision=lax.Precision.HIGHEST,
        preferred_element_type=jnp.float32,
    )
    plan[n_obs : 2 * n_obs, :n_obs] = link
    to_table = pltpu.make_async_copy(plan, table, plan_sem)
    to_table.start()
    to_table.wait()

    width = 8
    spread = width // mem_dev

    @pl.loop(0, n_slab)
    def _(s):
        pltpu.make_async_copy(
            blocks.at[s, pl.ds(0, n_mem - 1)], blocks.at[s, pl.ds(0, n_mem - 1)], out_recv.at[s]
        ).wait()

        def add_up(t, acc):
            for u in range(spread):
                for p in range(mem_dev):
                    acc = acc + blocks[s, t * spread + u, p]
            return acc

        zero = jnp.zeros((ROWS, LANES), jnp.float32)
        centre = lax.fori_loop(0, n_mem // spread, add_up, zero) * (1.0 / members)

        def solve(kb, base):
            k0 = kb * width

            def dots(t, acc):
                acc = list(acc)
                for u in range(spread):
                    i = t * spread + u
                    for p in range(mem_dev):
                        x = blocks[s, i, p] - centre
                        for e in range(width):
                            acc[e] = acc[e] + table[k0 + e, p * half + i] * x
                return tuple(acc)

            def links(jb, acc):
                acc = list(acc)
                for f in range(width):
                    j = jb * width + f
                    x = push[j]
                    for e in range(width):
                        acc[e] = acc[e] + table[n_obs + k0 + e, j] * x
                return tuple(acc)

            acc = lax.fori_loop(0, n_mem // spread, dots, (zero,) * width)
            acc = list(lax.fori_loop(0, kb, links, acc))
            for e in range(width):
                k = k0 + e
                w = (cell_loc[k] * table[2 * n_obs + k, 2]) * acc[e]
                pushed = table[2 * n_obs + k, 0] * w
                base = base + table[2 * n_obs + k, 1] * w
                push[k] = pushed
                for f in range(e + 1, width):
                    acc[f] = acc[f] + table[n_obs + k0 + f, k] * pushed
            return base

        base = lax.fori_loop(0, n_obs // width, solve, zero)

        @pl.loop(0, n_mem // spread)
        def _(t):
            own = [lax.rem(me + t * spread + u, n_mem) for u in range(spread)]
            at = [(i, p) for i in own for p in range(mem_dev)]

            def apply(kb, acc):
                acc = list(acc)
                for e in range(width):
                    k = kb * width + e
                    x = push[k]
                    for g, (i, p) in enumerate(at):
                        acc[g] = acc[g] + table[k, p * half + i] * x
                return tuple(acc)

            acc = lax.fori_loop(
                0, n_obs // width, apply, tuple(blocks[s, i, p] + base for i, p in at)
            )
            for g, (i, p) in enumerate(at):
                blocks[s, i, p] = acc[g]
            for u in range(spread):

                @pl.when(t * spread + u > 0)
                def _():
                    pltpu.make_async_remote_copy(
                        src_ref=blocks.at[s, own[u]],
                        dst_ref=tile_of(out, (slice(None), s), me),
                        send_sem=back_send,
                        recv_sem=back_recv,
                        device_id={"mem": own[u]},
                        device_id_type=MESH,
                    ).start()

    def own_copy(s):
        return pltpu.make_async_copy(
            blocks.at[s, me], tile_of(out, (slice(None), s), me), own_sem.at[s]
        )

    @pl.loop(0, n_slab)
    def _(s):
        own_copy(s).start()

    others = blocks.at[:, pl.ds(0, n_mem - 1)]

    @pl.loop(0, n_slab)
    def _(s):
        sent = blocks.at[s, pl.ds(0, n_mem - 1)]
        pltpu.make_async_copy(sent, sent, out_send.at[s]).wait()
        own_copy(s).wait()

    pltpu.make_async_copy(lev_rows(n_lev - 1), lev_rows(n_lev - 1), lev_send).wait()
    pltpu.make_async_copy(
        got_mem.at[pl.ds(0, n_mem - 1)], got_mem.at[pl.ds(0, n_mem - 1)], mem_send
    ).wait()
    pltpu.make_async_copy(others, others, back_send).wait()
    pltpu.make_async_copy(others, others, back_recv).wait()


def body(prior, vert, horz, diff, cells, slabs, vals, errs):
    n_mem, n_lev = lax.axis_size("mem"), lax.axis_size("lev")
    mem_dev, n_slab, grid_rows, grid_cols = prior.shape
    n_obs = cells.size
    f32 = jnp.float32
    whole = pl.BlockSpec(memory_space=pl.ANY)
    scalars = pl.BlockSpec(memory_space=pltpu.SMEM)
    dma = pltpu.SemaphoreType.DMA
    return pl.pallas_call(
        functools.partial(kernel, n_mem, n_lev),
        out_shape=jax.ShapeDtypeStruct(prior.shape, prior.dtype),
        in_specs=[whole] * 3 + [scalars] * 5,
        out_specs=whole,
        scratch_shapes=[
            pltpu.VMEM((n_slab, mem_dev, grid_rows, grid_cols), f32),
            pltpu.VMEM((n_slab, grid_rows, grid_cols), f32),
            pltpu.VMEM((n_slab, grid_rows, grid_cols), f32),
            pltpu.VMEM((4, grid_rows, grid_cols), f32),
            pltpu.VMEM((n_slab, mem_dev, grid_rows, grid_cols), f32),
            pltpu.VMEM((n_slab, n_mem, mem_dev, ROWS, LANES), f32),
            pltpu.VMEM((n_lev, 1, LANES), f32),
            pltpu.VMEM((n_mem, 1, LANES), f32),
            pltpu.VMEM((2, 1, LANES), f32),
            pltpu.VMEM((mem_dev, n_obs, LANES), f32),
            pltpu.VMEM((LANES, LANES), f32),
            pltpu.VMEM((n_obs, LANES), f32),
            pltpu.VMEM((n_obs, LANES), f32),
            pltpu.VMEM((n_obs, n_obs, LANES), f32),
            pltpu.VMEM((2, n_obs, LANES), f32),
            pltpu.VMEM((3 * n_obs, LANES), f32),
            pltpu.SMEM((3 * n_obs, LANES), f32),
            pltpu.VMEM((n_obs, ROWS, LANES), f32),
            pltpu.VMEM((n_obs, ROWS, LANES), f32),
            dma((3, n_slab)),
            dma,
            dma,
            dma,
            dma,
            dma((n_slab,)),
            dma((n_slab,)),
            dma,
            dma,
            dma,
            dma((n_slab,)),
        ],
        compiler_params=pltpu.CompilerParams(
            collective_id=0, has_side_effects=True, vmem_limit_bytes=40 << 20
        ),
        name="filter_cycle",
    )(prior, vert, horz, diff, cells, slabs, vals, errs)


def solution(mesh):
    in_specs = (
        P("mem", "lev", None, None),
        P("lev", None, None),
        P("lev", None, None),
        P("lev"),
        P(),
        P(),
        P(),
        P(),
    )
    out_specs = P("mem", "lev", None, None)
    return jax.shard_map(body, mesh=mesh, in_specs=in_specs, out_specs=out_specs, check_vma=False)
```

time: 890 us -> 93 us (0.10)
  local copies, waits for them, and re-layouts: 278 us -> 7.92 us
  loops' own time: 254 us -> 0 us
  blocking collectives: 205 us -> 0 us
  Pallas kernels: 0 us -> 84.4 us
  other arithmetic: 77.4 us -> 0 us
  waiting for transfers between devices: 33.2 us -> 0 us
  matrix products: 25.7 us -> 0 us
  starting transfers between devices: 11.5 us -> 0 us
    another operation x4 -> x0, loops' own time: 254 us -> none  [the longest x2 191 us: obs_space(): prior_rows, obs_plan = lax.scan(advance_obs, prior_rows, positions)]
    psum x2 -> x0, blocking collectives: 147 us -> none  [body(): prior_rows = lax.psum(partial_value, ('mem', 'lev'))]
    unnamed x14 -> x17, local copies, waits for them, and re-layouts: 112 us -> 7.92 us
    dynamic_slice x224 -> x0, local copies, waits for them, and re-layouts: 95.1 us -> none  [the longest x64 37.4 us: obs_space(): prior_rows, obs_plan = lax.scan(advance_obs, prior_rows, positions)]
    pallas_call x0 -> x1, Pallas kernels: none -> 84.4 us  [body(): pl.pallas_call(functools.partial(kernel, n_mem, n_lev), out_shape=jax.Sha...]
    all_to_all x1 -> x0, blocking collectives: 57.4 us -> none  [body(): lax.all_to_all(state_rows, 'mem', split_axis=0, concat_axis=2, tiled=True)]
    reduce_sum x99 -> x0, other arithmetic: 43 us -> none  [the longest x32 19.5 us: advance_obs(): spread = jnp.sum(anomaly * anomaly) / (member_count - 1) + 1e-06]
    all_to_all x6 -> x0, local copies, waits for them, and re-layouts: 34.3 us -> none  [the longest x5 33.6 us: body(): lax.all_to_all(by_cells, 'mem', split_axis=2, concat_axis=0, tiled=True)]
  transfers between devices with their start and end apart: 1 -> 0, of which waited for: 1 -> 0; matrix products, arithmetic and copies ran while one was open for 0% -> 0% of each run, Pallas kernels for 0% -> 0%
where the time goes in v1:
time: 93 us; the launch traced here: 92.3 us
  Pallas kernels  84.4 us (91%)
  local copies, waits for them, and re-layouts  7.92 us (9%)
    pallas_call x1, Pallas kernels, body(): pl.pallas_call(functools.partial(kernel, n_mem, n_lev), out_shape=jax.Sha...  84.4 us
    unnamed x17, local copies, waits for them, and re-layouts  7.92 us

profile of v1, /device:TPU:32, one launch (start us, length us, event | category | flops | bytes accessed | tf_op | source)
XLA Modules:
  0.0 92.3 jit_solution(1164392085083357664)
XLA Ops:
  0.0 0.0 copy-start
  0.0 1.3 %copy-done = f32[2,5,64,512]{3,2,1,0:T(8,128)S(1)} copy-done((f32[2,5,64,512]{3,2,1,0:T(8,128)S(1)}, f32[2,5,64,512]{3,2,1,0:T(8,128)}, u32[]{:S(2)}) %copy-start) | copy-done | bytes 1310744
  1.3 0.0 copy-start.1
  1.3 1.1 %copy-done.1 = f32[5,64,512]{2,1,0:T(8,128)S(1)} copy-done((f32[5,64,512]{2,1,0:T(8,128)S(1)}, f32[5,64,512]{2,1,0:T(8,128)}, u32[]{:S(2)}) %copy-start.1) | copy-done | bytes 655384
  2.4 0.0 copy-start.2
  2.4 1.1 %copy-done.2 = f32[5,64,512]{2,1,0:T(8,128)S(1)} copy-done((f32[5,64,512]{2,1,0:T(8,128)S(1)}, f32[5,64,512]{2,1,0:T(8,128)}, u32[]{:S(2)}) %copy-start.2) | copy-done | bytes 655384
  3.5 0.0 copy-start.3
  3.5 0.7 copy-done.3
  4.2 0.0 copy-start.4
  4.2 0.7 copy-done.4
  4.9 0.0 copy-start.5
  4.9 0.7 copy-done.5
  5.5 0.0 copy-start.6
  5.5 0.7 copy-done.6
  6.2 0.0 copy-start.7
  6.2 0.7 copy-done.7
  6.9 84.4 %filter_cycle.1 = f32[2,5,64,512]{3,2,1,0:T(8,128)S(1)} custom-call(f32[2,5,64,512]{3,2,1,0:T(8,128)S(1)} %copy-done, f32[5,64,512]{2,1,0:T(8,128)S(1)} %copy-done.1, f32[5,64,512]{2,1,0:T(8,128)S(1)} %copy-done.2, f32[5]{0:T(128)S(1)} %copy-done.7, s32[2,16]{1,0:T(2,128)S(1)} %copy-done.3, s32[2,16]{1,0:T(2,128)S(1)} %copy-done.4, f32[2,16]{1,0:T(2,128)S(1)} %copy-done.5, ...), custom_call_target="tpu_custom_call" | custom-call | tf_op jit(solution)/shard_map/filter_cycle/pallas_call | solution.py:440
  91.3 1.1 %copy.10 = f32[2,5,64,512]{3,2,1,0:T(8,128)} copy(f32[2,5,64,512]{3,2,1,0:T(8,128)S(1)} %filter_cycle.1) | data formatting | bytes 2621440
Async XLA Ops:
  0.0 1.3 %copy-start = (f32[2,5,64,512]{3,2,1,0:T(8,128)S(1)}, f32[2,5,64,512]{3,2,1,0:T(8,128)}, u32[]{:S(2)}) copy-start(f32[2,5,64,512]{3,2,1,0:T(8,128)} %prior.1) | copy-start | bytes 3932164
  1.3 1.1 %copy-start.1 = (f32[5,64,512]{2,1,0:T(8,128)S(1)}, f32[5,64,512]{2,1,0:T(8,128)}, u32[]{:S(2)}) copy-start(f32[5,64,512]{2,1,0:T(8,128)} %vert.1) | copy-start | bytes 1966084
  2.4 1.1 %copy-start.2 = (f32[5,64,512]{2,1,0:T(8,128)S(1)}, f32[5,64,512]{2,1,0:T(8,128)}, u32[]{:S(2)}) copy-start(f32[5,64,512]{2,1,0:T(8,128)} %horz.1) | copy-start | bytes 1966084
  3.5 0.7 copy-start.3
  4.2 0.7 copy-start.4
  4.9 0.7 copy-start.5
  5.5 0.7 copy-start.6
  6.2 0.7 copy-start.7

commit v2 on v1

--- a/solution.py
+++ b/solution.py
@@ -36,12 +36,17 @@
     prior,
     vert,
     horz,
+    diff_in,
+    cells_in,
+    slabs_in,
+    vals_in,
+    errs_in,
+    out,
     diff,
     cells,
     slabs,
     vals,
     errs,
-    out,
     pin,
     vin,
     hin,
@@ -60,8 +65,16 @@
     plan,
     table,
     cell_loc,
+    ys,
+    wide,
+    tall,
+    spread_in,
+    spread_out,
+    centred,
+    cross,
     push,
     in_sem,
+    obs_sem,
     lev_send,
     lev_recv,
     mem_send,
@@ -95,6 +108,21 @@
             pltpu.make_async_copy(horz.at[s], hin.at[s], in_sem.at[2, s]),
         )
 
+    small = [
+        pltpu.make_async_copy(a, b, obs_sem.at[i])
+        for i, (a, b) in enumerate(
+            (
+                (diff_in, diff),
+                (cells_in, cells),
+                (slabs_in, slabs),
+                (vals_in, vals),
+                (errs_in, errs),
+            )
+        )
+    ]
+    for copy in small:
+        copy.start()
+
     @pl.loop(0, n_slab)
     def _(s):
         for copy in fetch(s):
@@ -165,6 +193,8 @@
                 device_id_type=MESH,
             ).start()
 
+    for copy in small:
+        copy.wait()
     forecast(0)
     pl.semaphore_wait(barrier, n_mem - 1 + n_lev - 1)
     send_blocks(0)
@@ -300,26 +330,62 @@
         c = obs_loc[k] * g * gain
         anom[...] = every + (c * less) * a
         mean[...] = mean[...] + c * move
-        plan[pl.ds(k, 1), :] = a
-        plan[pl.ds(2 * n_obs + k, 1), :] = jnp.where(
+        ys[pl.ds(k, 1), :] = a
+        plan[pl.ds(n_obs + k, 1), :] = jnp.where(
             lane1 == 0, less, jnp.where(lane1 == 1, move, gain)
         )
 
-    y = plan[:n_obs]
-    link = lax.dot_general(
-        y,
-        y,
-        (((1,), (1,)), ((), ())),
-        precision=lax.Precision.HIGHEST,
-        preferred_element_type=jnp.float32,
+    def product(a, b, axis=0):
+        return lax.dot_general(
+            a,
+            b,
+            (((1,), (axis,)), ((), ())),
+            precision=lax.Precision.HIGHEST,
+            preferred_element_type=jnp.float32,
+        )
+
+    y = ys[...]
+    plan[:n_obs, :n_obs] = product(y, y, 1)
+    square[:n_obs, :] = y
+    square[n_obs:, :] = jnp.zeros((LANES - n_obs, LANES), jnp.float32)
+    turned = square[...].T
+    at = lax.broadcasted_iota(jnp.int32, (LANES, members * ROWS), 1) // ROWS
+    lane_of = lax.rem(at, mem_dev) * half + at // mem_dev
+    pick_in = (lane_of == lax.broadcasted_iota(jnp.int32, (LANES, members * ROWS), 0)).astype(
+        jnp.float32
     )
-    plan[n_obs : 2 * n_obs, :n_obs] = link
+    wide[...] = product(y, pick_in)
+    pick_out = (
+        lax.broadcasted_iota(jnp.int32, (LANES, n_obs * ROWS), 1) // ROWS
+        == lax.broadcasted_iota(jnp.int32, (LANES, n_obs * ROWS), 0)
+    ).astype(jnp.float32)
+    tall[...] = product(turned, pick_out)
+
+    def same_row(n):
+        shape = (ROWS, n * ROWS)
+        return lax.rem(lax.broadcasted_iota(jnp.int32, shape, 1), ROWS) == (
+            lax.broadcasted_iota(jnp.int32, shape, 0)
+        )
+
+    @pl.loop(0, n_obs)
+    def _(k):
+        spread_in[pl.ds(pl.multiple_of(k * ROWS, ROWS), ROWS), :] = jnp.where(
+            same_row(members), wide[pl.ds(k, 1), :], 0.0
+        )
+
+    @pl.loop(0, n_mem)
+    def _(i):
+        for p in range(mem_dev):
+            at = pl.multiple_of((i * mem_dev + p) * ROWS, ROWS)
+            spread_out[pl.ds(at, ROWS), :] = jnp.where(
+                same_row(n_obs), tall[pl.ds(p * half + i, 1), :], 0.0
+            )
+
     to_table = pltpu.make_async_copy(plan, table, plan_sem)
     to_table.start()
     to_table.wait()
 
     width = 8
-    spread = width // mem_dev
 
     @pl.loop(0, n_slab)
     def _(s):
@@ -327,27 +393,13 @@
             blocks.at[s, pl.ds(0, n_mem - 1)], blocks.at[s, pl.ds(0, n_mem - 1)], out_recv.at[s]
         ).wait()
 
-        def add_up(t, acc):
-            for u in range(spread):
-                for p in range(mem_dev):
-                    acc = acc + blocks[s, t * spread + u, p]
-            return acc
-
-        zero = jnp.zeros((ROWS, LANES), jnp.float32)
-        centre = lax.fori_loop(0, n_mem // spread, add_up, zero) * (1.0 / members)
+        x = blocks[s].reshape(members, ROWS, LANES)
+        centre = jnp.sum(x, axis=0) * (1.0 / members)
+        centred[...] = (x - centre).reshape(members * ROWS, LANES)
+        cross[...] = product(spread_in[...], centred[...]).reshape(n_obs, ROWS, LANES)
 
         def solve(kb, base):
             k0 = kb * width
-
-            def dots(t, acc):
-                acc = list(acc)
-                for u in range(spread):
-                    i = t * spread + u
-                    for p in range(mem_dev):
-                        x = blocks[s, i, p] - centre
-                        for e in range(width):
-                            acc[e] = acc[e] + table[k0 + e, p * half + i] * x
-                return tuple(acc)
 
             def links(jb, acc):
                 acc = list(acc)
@@ -355,54 +407,37 @@
                     j = jb * width + f
                     x = push[j]
                     for e in range(width):
-                        acc[e] = acc[e] + table[n_obs + k0 + e, j] * x
+                        acc[e] = acc[e] + table[k0 + e, j] * x
                 return tuple(acc)
 
-            acc = lax.fori_loop(0, n_mem // spread, dots, (zero,) * width)
+            acc = tuple(cross[k0 + e] for e in range(width))
             acc = list(lax.fori_loop(0, kb, links, acc))
             for e in range(width):
                 k = k0 + e
-                w = (cell_loc[k] * table[2 * n_obs + k, 2]) * acc[e]
-                pushed = table[2 * n_obs + k, 0] * w
-                base = base + table[2 * n_obs + k, 1] * w
+                w = (cell_loc[k] * table[n_obs + k, 2]) * acc[e]
+                pushed = table[n_obs + k, 0] * w
+                base = base + table[n_obs + k, 1] * w
                 push[k] = pushed
                 for f in range(e + 1, width):
-                    acc[f] = acc[f] + table[n_obs + k0 + f, k] * pushed
+                    acc[f] = acc[f] + table[k0 + f, k] * pushed
             return base
 
-        base = lax.fori_loop(0, n_obs // width, solve, zero)
-
-        @pl.loop(0, n_mem // spread)
-        def _(t):
-            own = [lax.rem(me + t * spread + u, n_mem) for u in range(spread)]
-            at = [(i, p) for i in own for p in range(mem_dev)]
-
-            def apply(kb, acc):
-                acc = list(acc)
-                for e in range(width):
-                    k = kb * width + e
-                    x = push[k]
-                    for g, (i, p) in enumerate(at):
-                        acc[g] = acc[g] + table[k, p * half + i] * x
-                return tuple(acc)
-
-            acc = lax.fori_loop(
-                0, n_obs // width, apply, tuple(blocks[s, i, p] + base for i, p in at)
-            )
-            for g, (i, p) in enumerate(at):
-                blocks[s, i, p] = acc[g]
-            for u in range(spread):
-
-                @pl.when(t * spread + u > 0)
-                def _():
-                    pltpu.make_async_remote_copy(
-                        src_ref=blocks.at[s, own[u]],
-                        dst_ref=tile_of(out, (slice(None), s), me),
-                        send_sem=back_send,
-                        recv_sem=back_recv,
-                        device_id={"mem": own[u]},
-                        device_id_type=MESH,
-                    ).start()
+        base = lax.fori_loop(0, n_obs // width, solve, jnp.zeros((ROWS, LANES), jnp.float32))
+        moved = product(spread_out[...], push[...].reshape(n_obs * ROWS, LANES))
+        moved = moved.reshape(members, ROWS, LANES) + base
+        blocks[s] = blocks[s] + moved.reshape(n_mem, mem_dev, ROWS, LANES)
+
+        @pl.loop(1, n_mem)
+        def _(i):
+            d = lax.rem(me + i, n_mem)
+            pltpu.make_async_remote_copy(
+                src_ref=blocks.at[s, d],
+                dst_ref=tile_of(out, (slice(None), s), me),
+                send_sem=back_send,
+                recv_sem=back_recv,
+                device_id={"mem": d},
+                device_id_type=MESH,
+            ).start()
 
     def own_copy(s):
         return pltpu.make_async_copy(
@@ -433,16 +468,21 @@
     n_mem, n_lev = lax.axis_size("mem"), lax.axis_size("lev")
     mem_dev, n_slab, grid_rows, grid_cols = prior.shape
     n_obs = cells.size
+    members = mem_dev * n_mem
     f32 = jnp.float32
     whole = pl.BlockSpec(memory_space=pl.ANY)
-    scalars = pl.BlockSpec(memory_space=pltpu.SMEM)
     dma = pltpu.SemaphoreType.DMA
     return pl.pallas_call(
         functools.partial(kernel, n_mem, n_lev),
         out_shape=jax.ShapeDtypeStruct(prior.shape, prior.dtype),
-        in_specs=[whole] * 3 + [scalars] * 5,
+        in_specs=[whole] * 8,
         out_specs=whole,
         scratch_shapes=[
+            pltpu.SMEM(diff.shape, diff.dtype),
+            pltpu.SMEM(cells.shape, cells.dtype),
+            pltpu.SMEM(slabs.shape, slabs.dtype),
+            pltpu.SMEM(vals.shape, vals.dtype),
+            pltpu.SMEM(errs.shape, errs.dtype),
             pltpu.VMEM((n_slab, mem_dev, grid_rows, grid_cols), f32),
             pltpu.VMEM((n_slab, grid_rows, grid_cols), f32),
             pltpu.VMEM((n_slab, grid_rows, grid_cols), f32),
@@ -458,11 +498,19 @@
             pltpu.VMEM((n_obs, LANES), f32),
             pltpu.VMEM((n_obs, n_obs, LANES), f32),
             pltpu.VMEM((2, n_obs, LANES), f32),
-            pltpu.VMEM((3 * n_obs, LANES), f32),
-            pltpu.SMEM((3 * n_obs, LANES), f32),
+            pltpu.VMEM((2 * n_obs, LANES), f32),
+            pltpu.SMEM((2 * n_obs, LANES), f32),
+            pltpu.VMEM((n_obs, ROWS, LANES), f32),
+            pltpu.VMEM((n_obs, LANES), f32),
+            pltpu.VMEM((n_obs, members * ROWS), f32),
+            pltpu.VMEM((LANES, n_obs * ROWS), f32),
+            pltpu.VMEM((n_obs * ROWS, members * ROWS), f32),
+            pltpu.VMEM((members * ROWS, n_obs * ROWS), f32),
+            pltpu.VMEM((members * ROWS, LANES), f32),
             pltpu.VMEM((n_obs, ROWS, LANES), f32),
             pltpu.VMEM((n_obs, ROWS, LANES), f32),
             dma((3, n_slab)),
+            dma((5,)),
             dma,
             dma,
             dma,
@@ -475,7 +523,7 @@
             dma((n_slab,)),
         ],
         compiler_params=pltpu.CompilerParams(
-            collective_id=0, has_side_effects=True, vmem_limit_bytes=40 << 20
+            collective_id=0, has_side_effects=True, vmem_limit_bytes=62 << 20
         ),
         name="filter_cycle",
     )(prior, vert, horz, diff, cells, slabs, vals, errs)

time: 93 us -> 71.6 us (0.77)
  Pallas kernels: 84.4 us -> 67.9 us
  local copies, waits for them, and re-layouts: 7.92 us -> 2.47 us
    pallas_call x1, Pallas kernels: 84.4 us -> 67.9 us  [body(): pl.pallas_call(functools.partial(kernel, n_mem, n_lev), out_shape=jax.Sha...]
    unnamed x17 -> x1, local copies, waits for them, and re-layouts: 7.92 us -> 2.47 us
where the time goes in v2:
time: 71.6 us; the launch traced here: 70.4 us
  Pallas kernels  67.9 us (95%)
  local copies, waits for them, and re-layouts  2.47 us (3%)
    pallas_call x1, Pallas kernels, body(): pl.pallas_call(functools.partial(kernel, n_mem, n_lev), out_shape=jax.Sha...  67.9 us
    unnamed x1, local copies, waits for them, and re-layouts  2.47 us

profile of v2, /device:TPU:32, one launch (start us, length us, event | category | flops | bytes accessed | tf_op | source)
XLA Modules:
  0.0 70.4 jit_solution(4456354015717583061)
XLA Ops:
  0.0 67.9 %filter_cycle.1 = f32[2,5,64,512]{3,2,1,0:T(8,128)} custom-call(f32[2,5,64,512]{3,2,1,0:T(8,128)} %prior.1, f32[5,64,512]{2,1,0:T(8,128)} %vert.1, f32[5,64,512]{2,1,0:T(8,128)} %horz.1, f32[5]{0:T(128)} %diff_in.1, s32[2,16]{1,0:T(2,128)} %cells_in.1, s32[2,16]{1,0:T(2,128)} %slabs_in.1, f32[2,16]{1,0:T(2,128)} %vals_in.1, f32[2,16]{1,0:T(2,128)} %errs_in.1), custom_call_target="tpu_custom_call" | custom-call | tf_op jit(solution)/shard_map/filter_cycle/pallas_call | solution.py:475
  68.0 2.5 %copy.10 = f32[2,5,64,512]{3,2,1,0:T(8,128)} copy(f32[2,5,64,512]{3,2,1,0:T(8,128)} %filter_cycle.1) | data formatting | bytes 2621440

commit v3 on v2

--- a/solution.py
+++ b/solution.py
@@ -12,7 +12,9 @@
 LOC_HALF = 64
 MESH = pl.DeviceIdType.MESH
 ROWS, LANES = 8, 128
-EARLY = 2
+RING = 8
+MIDDLE = 2
+EARLY = 1
 
 
 def taper(dist):
@@ -101,6 +103,20 @@
         c = pl.multiple_of((d % tiles_across) * LANES, LANES)
         return ref.at[lead + (pl.ds(r, ROWS), pl.ds(c, LANES))]
 
+    def peers(send):
+        y, z = me // RING, lax.rem(me, RING)
+
+        @pl.loop(0, n_mem // RING)
+        def _(j):
+            ahead = lax.rem(y + n_mem // RING - 1 - j, n_mem // RING) * RING
+            for t in range(RING):
+                step = RING // 2 + (t // 2 if t % 2 == 0 else -(t + 1) // 2)
+                d = ahead + lax.rem(z + step, RING)
+                if step > 0:
+                    send(d)
+                else:
+                    pl.when(j < n_mem // RING - 1)(functools.partial(send, d))
+
     def fetch(s):
         return (
             pltpu.make_async_copy(prior.at[:, s], pin.at[s], in_sem.at[0, s]),
@@ -181,9 +197,8 @@
                 pl.ds(pl.multiple_of(tile_col * LANES, LANES), LANES),
             ]
 
-        @pl.loop(1, n_mem)
-        def _(i):
-            d = lax.rem(me + i, n_mem)
+        @peers
+        def _(d):
             pltpu.make_async_remote_copy(
                 src_ref=tile_of(field, (s, slice(None)), d),
                 dst_ref=blocks.at[s, me],
@@ -238,12 +253,45 @@
             jnp.where(lane32 == sub32 + p * half, column, 0.0), axis=0, keepdims=True
         )
     msg[0] = share
-    got_lev[lev] = share
+    got_mem[me] = share
+
+    @peers
+    def _(d):
+        pltpu.make_async_remote_copy(
+            src_ref=msg.at[0],
+            dst_ref=got_mem.at[me],
+            send_sem=mem_send,
+            recv_sem=mem_recv,
+            device_id={"mem": d},
+            device_id_type=MESH,
+        ).start()
+
+    @pl.loop(EARLY, MIDDLE)
+    def _(s):
+        send_blocks(s)
+
+    cell_row = (
+        tile_row * ROWS + lax.broadcasted_iota(jnp.int32, (ROWS, LANES), 0)
+    ).astype(jnp.float32)
+    cell_col = (
+        tile_col * LANES + lax.broadcasted_iota(jnp.int32, (ROWS, LANES), 1)
+    ).astype(jnp.float32)
+
+    def lev_rows(copies):
+        return got_lev.at[pl.ds(0, copies)]
+
+    pltpu.make_async_copy(
+        got_mem.at[pl.ds(0, n_mem - 1)], got_mem.at[pl.ds(0, n_mem - 1)], mem_recv
+    ).wait()
+
+    @pl.loop(0, n_mem)
+    def _(i):
+        got_lev[lev, pl.ds(i, 1), :] = got_mem[i]
 
     @pl.loop(1, n_lev)
     def _(i):
         pltpu.make_async_remote_copy(
-            src_ref=msg.at[0],
+            src_ref=got_lev.at[lev],
             dst_ref=got_lev.at[lev],
             send_sem=lev_send,
             recv_sem=lev_recv,
@@ -251,35 +299,7 @@
             device_id_type=MESH,
         ).start()
 
-    cell_row = (
-        tile_row * ROWS + lax.broadcasted_iota(jnp.int32, (ROWS, LANES), 0)
-    ).astype(jnp.float32)
-    cell_col = (
-        tile_col * LANES + lax.broadcasted_iota(jnp.int32, (ROWS, LANES), 1)
-    ).astype(jnp.float32)
-
-    def lev_rows(copies):
-        return got_lev.at[pl.ds(0, copies)]
-
-    pltpu.make_async_copy(lev_rows(n_lev - 1), lev_rows(n_lev - 1), lev_recv).wait()
-    total = got_lev[0]
-    for i in range(1, n_lev):
-        total = total + got_lev[i]
-    msg[1] = total
-    got_mem[me] = total
-
-    @pl.loop(1, n_mem)
-    def _(i):
-        pltpu.make_async_remote_copy(
-            src_ref=msg.at[1],
-            dst_ref=got_mem.at[me],
-            send_sem=mem_send,
-            recv_sem=mem_recv,
-            device_id={"mem": lax.rem(me + i, n_mem)},
-            device_id_type=MESH,
-        ).start()
-
-    @pl.loop(EARLY, n_slab)
+    @pl.loop(MIDDLE, n_slab)
     def _(s):
         send_blocks(s)
 
@@ -294,15 +314,9 @@
         dr, dc = cell_row - r, cell_col - c
         cell_loc[k] = taper(jnp.sqrt(dr * dr + dc * dc))
 
-    square[...] = jnp.zeros_like(square)
-    pltpu.make_async_copy(
-        got_mem.at[pl.ds(0, n_mem - 1)], got_mem.at[pl.ds(0, n_mem - 1)], mem_recv
-    ).wait()
-
-    @pl.loop(0, n_mem)
-    def _(i):
-        square[pl.ds(i, 1), :] = got_mem[i]
-
+    square[n_mem:, :] = jnp.zeros((LANES - n_mem, LANES), jnp.float32)
+    pltpu.make_async_copy(lev_rows(n_lev - 1), lev_rows(n_lev - 1), lev_recv).wait()
+    square[:n_mem, :] = jnp.sum(got_lev[...], axis=0)
     turned = square[...].T
     rows = turned[:n_obs]
     for p in range(1, mem_dev):
@@ -427,9 +441,8 @@
         moved = moved.reshape(members, ROWS, LANES) + base
         blocks[s] = blocks[s] + moved.reshape(n_mem, mem_dev, ROWS, LANES)
 
-        @pl.loop(1, n_mem)
-        def _(i):
-            d = lax.rem(me + i, n_mem)
+        @peers
+        def _(d):
             pltpu.make_async_remote_copy(
                 src_ref=blocks.at[s, d],
                 dst_ref=tile_of(out, (slice(None), s), me),
@@ -464,7 +477,8 @@
     pltpu.make_async_copy(others, others, back_recv).wait()
 
 
-def body(prior, vert, horz, diff, cells, slabs, vals, errs):
+def body(*operands):
+    prior, _, _, diff, cells, slabs, vals, errs = operands
     n_mem, n_lev = lax.axis_size("mem"), lax.axis_size("lev")
     mem_dev, n_slab, grid_rows, grid_cols = prior.shape
     n_obs = cells.size
@@ -489,9 +503,9 @@
             pltpu.VMEM((4, grid_rows, grid_cols), f32),
             pltpu.VMEM((n_slab, mem_dev, grid_rows, grid_cols), f32),
             pltpu.VMEM((n_slab, n_mem, mem_dev, ROWS, LANES), f32),
-            pltpu.VMEM((n_lev, 1, LANES), f32),
+            pltpu.VMEM((n_lev, n_mem, LANES), f32),
             pltpu.VMEM((n_mem, 1, LANES), f32),
-            pltpu.VMEM((2, 1, LANES), f32),
+            pltpu.VMEM((1, 1, LANES), f32),
             pltpu.VMEM((mem_dev, n_obs, LANES), f32),
             pltpu.VMEM((LANES, LANES), f32),
             pltpu.VMEM((n_obs, LANES), f32),
@@ -523,10 +537,10 @@
             dma((n_slab,)),
         ],
         compiler_params=pltpu.CompilerParams(
-            collective_id=0, has_side_effects=True, vmem_limit_bytes=62 << 20
+            collective_id=0, has_side_effects=True, vmem_limit_bytes=40 << 20
         ),
         name="filter_cycle",
-    )(prior, vert, horz, diff, cells, slabs, vals, errs)
+    )(*(pltpu.with_memory_space_constraint(a, pltpu.HBM) for a in operands))
 
 
 def solution(mesh):

time: 71.6 us -> 70.1 us (0.979); the launches traced: 70.4 us -> 70 us
  local copies, waits for them, and re-layouts: 2.47 us -> 1.06 us
  Pallas kernels: 67.9 us -> 68.9 us
    unnamed x1, local copies, waits for them, and re-layouts: 2.47 us -> 1.06 us
    pallas_call x1, Pallas kernels: 67.9 us -> 68.9 us  [body(): pl.pallas_call(functools.partial(kernel, n_mem, n_lev), out_shape=jax.Sha...]
where the time goes in v3:
time: 70.1 us; the launch traced here: 70 us
  Pallas kernels  68.9 us (98%)
  local copies, waits for them, and re-layouts  1.06 us (2%)
    pallas_call x1, Pallas kernels, body(): pl.pallas_call(functools.partial(kernel, n_mem, n_lev), out_shape=jax.Sha...  68.9 us

profile of v3, /device:TPU:32, one launch (start us, length us, event | category | flops | bytes accessed | tf_op | source)
XLA Modules:
  0.0 70.0 jit_solution(18078638484157071816)
XLA Ops:
  0.0 68.9 %filter_cycle.1 = f32[2,5,64,512]{3,2,1,0:T(8,128)S(1)} custom-call(f32[2,5,64,512]{3,2,1,0:T(8,128)} %prior.1, f32[5,64,512]{2,1,0:T(8,128)} %vert.1, f32[5,64,512]{2,1,0:T(8,128)} %horz.1, f32[5]{0:T(128)} %diff_in.1, s32[2,16]{1,0:T(2,128)} %cells_in.1, s32[2,16]{1,0:T(2,128)} %slabs_in.1, f32[2,16]{1,0:T(2,128)} %vals_in.1, f32[2,16]{1,0:T(2,128)} %errs_in.1), custom_call_target="tpu_custom_call" | custom-call | tf_op jit(solution)/shard_map/filter_cycle/pallas_call | solution.py:489
  68.9 1.1 %copy.10 = f32[2,5,64,512]{3,2,1,0:T(8,128)} copy(f32[2,5,64,512]{3,2,1,0:T(8,128)S(1)} %filter_cycle.1) | data formatting | bytes 2621440

commit v4 on v3

--- a/solution.py
+++ b/solution.py
@@ -99,19 +99,33 @@
     tile_row, tile_col = me // tiles_across, me % tiles_across
 
     def tile_of(ref, lead, d):
-        r = pl.multiple_of((d // tiles_across) * ROWS, ROWS)
-        c = pl.multiple_of((d % tiles_across) * LANES, LANES)
+        r = pl.multiple_of(lax.div(d, tiles_across) * ROWS, ROWS)
+        c = pl.multiple_of(jnp.bitwise_and(d, tiles_across - 1) * LANES, LANES)
         return ref.at[lead + (pl.ds(r, ROWS), pl.ds(c, LANES))]
 
+    barrier = pltpu.get_barrier_semaphore()
+
+    @pl.loop(1, n_mem)
+    def _(i):
+        pl.semaphore_signal(
+            barrier, inc=1, device_id={"mem": jnp.bitwise_and(me + i, n_mem - 1)}, device_id_type=MESH
+        )
+
+    @pl.loop(1, n_lev)
+    def _(i):
+        pl.semaphore_signal(
+            barrier, inc=1, device_id={"lev": jnp.bitwise_and(lev + i, n_lev - 1)}, device_id_type=MESH
+        )
+
     def peers(send):
-        y, z = me // RING, lax.rem(me, RING)
+        y, z = lax.div(me, RING), jnp.bitwise_and(me, RING - 1)
 
         @pl.loop(0, n_mem // RING)
         def _(j):
-            ahead = lax.rem(y + n_mem // RING - 1 - j, n_mem // RING) * RING
+            ahead = jnp.bitwise_and(y - 1 - j, n_mem // RING - 1) * RING
             for t in range(RING):
                 step = RING // 2 + (t // 2 if t % 2 == 0 else -(t + 1) // 2)
-                d = ahead + lax.rem(z + step, RING)
+                d = ahead + jnp.bitwise_and(z + step, RING - 1)
                 if step > 0:
                     send(d)
                 else:
@@ -136,27 +150,15 @@
             )
         )
     ]
+    for copy in fetch(0):
+        copy.start()
     for copy in small:
         copy.start()
 
-    @pl.loop(0, n_slab)
+    @pl.loop(1, n_slab)
     def _(s):
         for copy in fetch(s):
             copy.start()
-
-    barrier = pltpu.get_barrier_semaphore()
-
-    @pl.loop(1, n_mem)
-    def _(i):
-        pl.semaphore_signal(
-            barrier, inc=1, device_id={"mem": lax.rem(me + i, n_mem)}, device_id_type=MESH
-        )
-
-    @pl.loop(1, n_lev)
-    def _(i):
-        pl.semaphore_signal(
-            barrier, inc=1, device_id={"lev": lax.rem(lev + i, n_lev)}, device_id_type=MESH
-        )
 
     col = lax.broadcasted_iota(jnp.int32, (grid_rows, grid_cols), 1)
     row = lax.broadcasted_iota(jnp.int32, (grid_rows, grid_cols), 0)
@@ -295,7 +297,7 @@
             dst_ref=got_lev.at[lev],
             send_sem=lev_send,
             recv_sem=lev_recv,
-            device_id={"lev": lax.rem(lev + i, n_lev)},
+            device_id={"lev": jnp.bitwise_and(lev + i, n_lev - 1)},
             device_id_type=MESH,
         ).start()
 

time: 70.1 us -> 69.9 us (level)
  no operation moved by 1% of the time
where the time goes in v4:
time: 69.9 us; the launch traced here: 69.8 us
  Pallas kernels  68.7 us (98%)
  local copies, waits for them, and re-layouts  1.06 us (2%)
    pallas_call x1, Pallas kernels, body(): pl.pallas_call(functools.partial(kernel, n_mem, n_lev), out_shape=jax.Sha...  68.7 us

profile of v4, /device:TPU:32, one launch (start us, length us, event | category | flops | bytes accessed | tf_op | source)
XLA Modules:
  0.0 69.8 jit_solution(4872956361358229615)
XLA Ops:
  0.0 68.7 %filter_cycle.1 = f32[2,5,64,512]{3,2,1,0:T(8,128)S(1)} custom-call(f32[2,5,64,512]{3,2,1,0:T(8,128)} %prior.1, f32[5,64,512]{2,1,0:T(8,128)} %vert.1, f32[5,64,512]{2,1,0:T(8,128)} %horz.1, f32[5]{0:T(128)} %diff_in.1, s32[2,16]{1,0:T(2,128)} %cells_in.1, s32[2,16]{1,0:T(2,128)} %slabs_in.1, f32[2,16]{1,0:T(2,128)} %vals_in.1, f32[2,16]{1,0:T(2,128)} %errs_in.1), custom_call_target="tpu_custom_call" | custom-call | tf_op jit(solution)/shard_map/filter_cycle/pallas_call | solution.py:491
  68.7 1.1 %copy.10 = f32[2,5,64,512]{3,2,1,0:T(8,128)} copy(f32[2,5,64,512]{3,2,1,0:T(8,128)S(1)} %filter_cycle.1) | data formatting | bytes 2621440

commit v5 on v4

--- a/solution.py
+++ b/solution.py
@@ -401,6 +401,26 @@
     to_table.start()
     to_table.wait()
 
+    def planes(first, count, send):
+        y, z = me // RING, lax.rem(me, RING)
+
+        @pl.loop(0, n_mem // RING)
+        def _(j):
+            ahead = lax.rem(y + n_mem // RING - 1 - j, n_mem // RING) * RING
+            for t in range(count):
+                d = ahead + first + lax.rem(z + count // 2 + t, count)
+                pl.when(d != me)(functools.partial(send, d))
+
+    def send_back(s, d):
+        pltpu.make_async_remote_copy(
+            src_ref=blocks.at[s, d],
+            dst_ref=tile_of(out, (slice(None), s), me),
+            send_sem=back_send,
+            recv_sem=back_recv,
+            device_id={"mem": d},
+            device_id_type=MESH,
+        ).start()
+
     width = 8
 
     @pl.loop(0, n_slab)
@@ -443,16 +463,27 @@
         moved = moved.reshape(members, ROWS, LANES) + base
         blocks[s] = blocks[s] + moved.reshape(n_mem, mem_dev, ROWS, LANES)
 
-        @peers
-        def _(d):
-            pltpu.make_async_remote_copy(
-                src_ref=blocks.at[s, d],
-                dst_ref=tile_of(out, (slice(None), s), me),
-                send_sem=back_send,
-                recv_sem=back_recv,
-                device_id={"mem": d},
-                device_id_type=MESH,
-            ).start()
+        planes(0, 1, functools.partial(send_back, s))
+
+        @pl.when(jnp.logical_or(s < 4, jnp.bitwise_and(me, RING - 1) < 1))
+        def _():
+            planes(1, RING - 1, functools.partial(send_back, s))
+
+    @pl.loop(4, n_slab)
+    def _(s):
+        @pl.when(jnp.bitwise_and(me, RING - 1) >= 1)
+        def _():
+            planes(1, 1, functools.partial(send_back, s))
+
+        @pl.when(jnp.logical_and(jnp.bitwise_and(me, RING - 1) >= 1, jnp.bitwise_and(me, RING - 1) < 2))
+        def _():
+            planes(2, RING - 2, functools.partial(send_back, s))
+
+    @pl.when(jnp.bitwise_and(me, RING - 1) >= 2)
+    def _():
+        @pl.loop(4, n_slab)
+        def _(s):
+            planes(2, RING - 2, functools.partial(send_back, s))
 
     def own_copy(s):
         return pltpu.make_async_copy(

time: 69.9 us -> 70 us (level)
  no operation moved by 1% of the time
where the time goes in v5:
time: 70 us; the launch traced here: 69.5 us
  Pallas kernels  68.4 us (98%)
  local copies, waits for them, and re-layouts  1.06 us (2%)
    pallas_call x1, Pallas kernels, body(): pl.pallas_call(functools.partial(kernel, n_mem, n_lev), out_shape=jax.Sha...  68.4 us

profile of v5, /device:TPU:32, one launch (start us, length us, event | category | flops | bytes accessed | tf_op | source)
XLA Modules:
  0.0 69.5 jit_solution(6899526528465898559)
XLA Ops:
  0.0 68.4 %filter_cycle.1 = f32[2,5,64,512]{3,2,1,0:T(8,128)S(1)} custom-call(f32[2,5,64,512]{3,2,1,0:T(8,128)} %prior.1, f32[5,64,512]{2,1,0:T(8,128)} %vert.1, f32[5,64,512]{2,1,0:T(8,128)} %horz.1, f32[5]{0:T(128)} %diff_in.1, s32[2,16]{1,0:T(2,128)} %cells_in.1, s32[2,16]{1,0:T(2,128)} %slabs_in.1, f32[2,16]{1,0:T(2,128)} %vals_in.1, f32[2,16]{1,0:T(2,128)} %errs_in.1), custom_call_target="tpu_custom_call" | custom-call | tf_op jit(solution)/shard_map/filter_cycle/pallas_call | solution.py:522
  68.4 1.1 %copy.10 = f32[2,5,64,512]{3,2,1,0:T(8,128)} copy(f32[2,5,64,512]{3,2,1,0:T(8,128)S(1)} %filter_cycle.1) | data formatting | bytes 2621440
